TPU v7x, 128 devices: a whole 4x4x4 slice. The times are simulated.
128 devices in a mesh: seq: 8 (over x, y_hi), fsdp: 16 (over y_lo, z, core).
Axes of the slice: x: 4, y: 4 (y_hi: 2, y_lo: 2; y = y_hi * 2 + y_lo), z: 4, core: 2. Of those that a mesh axis runs over, the one named last changes fastest.
Arguments:
- patches: bfloat16 [16, 2048, 1152], P('fsdp'), may hold values from -6 to 6
- counts: int32 [16, 8], P('fsdp'), may hold values from 1 to 505, as said below
- starts: int32 [16, 8], P('fsdp'), may hold values from 0 to 1023, as said below
- embeds: bfloat16 [16, 1024, 2048], P('fsdp', 'seq'), may hold values from -6 to 6
- route_ids: int32 [16, 1024, 6], P('fsdp'), may hold values from 0 to 63, all different within a row; in each aligned block of 1024 rows (0 to 1023, 1024 to 2047, ..., all dimensions but the last counted through in order) at most 128 rows name the same one
- route_weights: float32 [16, 1024, 6], P('fsdp'), may hold values from 0.1 to 0.6
- vit_gain: float32 [1152], replicated, may hold values from 0.5 to 1.5
- vit_fc1: bfloat16 [1152, 4304], P('fsdp', 'seq'), may hold values from -0.1875 to 0.1875
- vit_fc2: bfloat16 [1152, 4304], P('fsdp', 'seq'), may hold values from -0.09375 to 0.09375
- proj_gain: float32 [4608], replicated, may hold values from 0.5 to 1.5
- proj_weight: bfloat16 [4608, 2048], P('fsdp', 'seq'), may hold values from -0.09375 to 0.09375
- moe_gain: float32 [2048], replicated, may hold values from 0.5 to 1.5
- shared_gate: bfloat16 [2048, 2816], P('fsdp', 'seq'), may hold values from -0.125 to 0.125
- shared_up: bfloat16 [2048, 2816], P('fsdp', 'seq'), may hold values from -0.125 to 0.125
- shared_down: bfloat16 [2048, 2816], P('fsdp', 'seq'), may hold values from -0.109375 to 0.109375
- expert_gate: bfloat16 [2048, 8, 1408], P('fsdp', 'seq'), may hold values from -0.125 to 0.125
- expert_up: bfloat16 [2048, 8, 1408], P('fsdp', 'seq'), may hold values from -0.125 to 0.125
- expert_down: bfloat16 [2048, 8, 1408], P('fsdp', 'seq'), may hold values from -0.15625 to 0.15625
Outputs:
- layer_out: bfloat16 [16, 1024, 2048], P('fsdp', 'seq')
Inputs may be any that keep to these rules, and one draw needn't show every extreme that they name: Per stream the counts of its 8 images sum to 512. `starts`: images of a stream lie in order in disjoint runs of positions inside its 1024 positions; in each stream the 128 positions of some one index of seq are all visual. `route_ids`: the 6 experts of a token differ; in each stream no expert is chosen by more than 128 tokens.
All inputs are finite; a program needn't handle non-finite values.
Results may differ from a plain program's by a relative error of at most 0.014.
Values may be sent and summed in bfloat16 or wider, within the bound.
No kernel may reach another device: no remote copies, remote signals or barrier semaphores. Data moves between devices by JAX's collectives and lax.ppermute only.
A program may use at most 128 MiB of HBM per device.

v0:
```python
import jax
import jax.numpy as jnp
from jax import lax
from jax.sharding import PartitionSpec as P

ln_epsilon = 1e-05
rms_epsilon = 1e-06


def sent_together(arrays, axis, dim, along):
    both = jnp.concatenate(arrays, axis=along)
    result, at, gathered = (lax.all_gather(both, axis, axis=dim, tiled=True), 0, [])
    for a in arrays:
        gathered.append(lax.slice_in_dim(result, at, at + a.shape[along], axis=along))
        at += a.shape[along]
    return tuple(gathered)


def rows_for(lines, count):
    spare = -len(lines) % count
    return jnp.pad(lines, [(0, spare)] + [(0, 0)] * (lines.ndim - 1))


def sum_in_two_steps(x, axis):
    lines = x.reshape(-1, *x.shape[1:][-1:])
    own = lax.psum_scatter(
        rows_for(lines, lax.axis_size(axis)), axis, scatter_dimension=0, tiled=True
    )
    whole = lax.all_gather(own, axis).reshape(-1, *lines.shape[1:])
    return lax.slice_in_dim(whole, 0, len(lines)).reshape(x.shape)


def in_one_piece(arrays, axis, dim, along):
    columns = [a.reshape(*a.shape[:along], -1) for a in arrays]
    both = jnp.concatenate(columns, axis=along)
    result, at, gathered = (lax.all_gather(both, axis, axis=dim, tiled=True), 0, [])
    for a, column in zip(arrays, columns):
        piece = result[..., at : at + column.shape[along]]
        gathered.append(piece.reshape(*piece.shape[:along], *a.shape[along:]))
        at += column.shape[along]
    return tuple(gathered)


def split_up(x, dim, count):
    shape = x.shape
    parts = x.reshape(*shape[:dim], count, shape[dim] // count, *shape[dim + 1 :])
    return jnp.moveaxis(parts, dim, 0)


def sum_at_owner(x, axis, dim):
    count = lax.axis_size(axis)
    parts = lax.all_to_all(split_up(x, dim, count), axis, 0, 0, tiled=True)
    return jnp.sum(parts.astype(jnp.float32), axis=0)


def layer_norm(values, gain_vec):
    center = values - jnp.mean(values, axis=-1, keepdims=True)
    spread = jnp.mean(center * center, axis=-1, keepdims=True)
    return center * lax.rsqrt(spread + ln_epsilon) * gain_vec


def rms_norm(values, gain_vec):
    square = jnp.mean(values * values, axis=-1, keepdims=True)
    return values * lax.rsqrt(square + rms_epsilon) * gain_vec


def visual_positions(counts, starts, total):
    end_index = jnp.cumsum(counts)
    begins = end_index - counts
    token_index = jnp.arange(total, dtype=jnp.int32)
    inside = (token_index[:, None] >= begins[None, :]) & (token_index[:, None] < end_index[None, :])
    placed = starts[None, :] + token_index[:, None] - begins[None, :]
    return jnp.sum(jnp.where(inside, placed, 0), axis=1)


def routed_rows(gathered, route_ids, route_weights, expert, capacity, gate_w, up_w, down_w):
    hit_mask = route_ids == expert
    chosen = jnp.any(hit_mask, axis=1)
    weight_sum = jnp.sum(jnp.where(hit_mask, route_weights, 0.0), axis=1)
    count_rows = gathered.shape[0]
    slot_rank = jnp.cumsum(chosen.astype(jnp.int32)) - 1
    target = jnp.where(chosen, slot_rank, capacity)
    slot_rows = (
        jnp.zeros((capacity,), jnp.int32)
        .at[target]
        .set(jnp.arange(count_rows, dtype=jnp.int32), mode="drop")
    )
    is_live = jnp.arange(capacity, dtype=jnp.int32) < jnp.sum(chosen.astype(jnp.int32))
    picked = jnp.take(gathered, slot_rows, axis=0)
    gate_part = jnp.dot(picked, gate_w, preferred_element_type=jnp.float32)
    up_part = jnp.dot(picked, up_w, preferred_element_type=jnp.float32)
    hidden = (jax.nn.silu(gate_part) * up_part).astype(jnp.bfloat16)
    result = lax.dot_general(
        hidden, down_w, (((1,), (1,)), ((), ())), preferred_element_type=jnp.float32
    )
    factor = jnp.where(is_live, jnp.take(weight_sum, slot_rows), 0.0)
    return (slot_rows, result * factor[:, None])


def shards(
    patches,
    counts,
    starts,
    embeds,
    route_ids,
    route_weights,
    vit_gain,
    vit_fc1,
    vit_fc2,
    proj_gain,
    proj_weight,
    moe_gain,
    shared_gate,
    shared_up,
    shared_down,
    expert_gate,
    expert_up,
    expert_down,
):
    seq_count = lax.axis_size("seq")
    seq_index = lax.axis_index("seq")
    vit_first, vit_second, projector = (
        *sent_together((vit_fc1, vit_fc2), "fsdp", 0, 1),
        lax.all_gather(proj_weight, "fsdp", axis=0, tiled=True),
    )
    image_rows = patches[0].astype(jnp.float32)
    normed = layer_norm(image_rows, vit_gain).astype(jnp.bfloat16)
    hidden = jax.nn.gelu(
        jnp.dot(normed, vit_first, preferred_element_type=jnp.float32), approximate=True
    ).astype(jnp.bfloat16)
    product = lax.dot_general(
        hidden, vit_second, (((1,), (1,)), ((), ())), preferred_element_type=jnp.float32
    )
    mixed_sum = sum_in_two_steps(product.astype(jnp.bfloat16), "seq").astype(jnp.float32)
    residual = image_rows + mixed_sum
    joined_width = residual.shape[1] * 4
    proj_in = layer_norm(residual.reshape(-1, joined_width), proj_gain).astype(jnp.bfloat16)
    visual = jnp.dot(proj_in, projector, preferred_element_type=jnp.float32).astype(jnp.bfloat16)
    tok_dev = embeds.shape[1]
    positions = visual_positions(counts[0], starts[0], visual.shape[0])
    owners = positions // tok_dev
    one_hot = (owners[:, None] == jnp.arange(seq_count, dtype=jnp.int32)[None, :]).astype(jnp.int32)
    slot_rank = jnp.sum((jnp.cumsum(one_hot, axis=0) - one_hot) * one_hot, axis=1)
    slot_index = owners * tok_dev + slot_rank
    send_buffer = (
        jnp.zeros((seq_count * tok_dev, visual.shape[1]), jnp.bfloat16).at[slot_index].set(visual)
    )
    received = lax.all_to_all(
        send_buffer.reshape(seq_count, tok_dev, visual.shape[1]),
        "seq",
        split_axis=0,
        concat_axis=2,
        tiled=True,
    )
    is_mine = owners == seq_index
    local_rows = positions % tok_dev
    slot_place = (
        jnp.full((tok_dev,), tok_dev, jnp.int32)
        .at[jnp.where(is_mine, slot_rank, tok_dev)]
        .set(local_rows, mode="drop")
    )
    merged = embeds[0].at[slot_place].set(received[0], mode="drop")
    normed_tokens = rms_norm(merged.astype(jnp.float32), moe_gain).astype(jnp.bfloat16)
    gathered = lax.all_gather(normed_tokens, "seq", axis=0, tiled=True)
    gate_shared, up_shared, down_shared, gate_expert, up_expert, down_expert = in_one_piece(
        (shared_gate, shared_up, shared_down, expert_gate, expert_up, expert_down), "fsdp", 0, 1
    )
    gate_part = jnp.dot(gathered, gate_shared, preferred_element_type=jnp.float32)
    up_part = jnp.dot(gathered, up_shared, preferred_element_type=jnp.float32)
    shared_hidden = (jax.nn.silu(gate_part) * up_part).astype(jnp.bfloat16)
    partial_value = lax.dot_general(
        shared_hidden, down_shared, (((1,), (1,)), ((), ())), preferred_element_type=jnp.float32
    )
    capacity = gathered.shape[0] // 8
    local_count = gate_expert.shape[1]
    expert = seq_index * local_count + 0
    slot_rows, values = routed_rows(
        gathered,
        route_ids[0],
        route_weights[0],
        expert,
        capacity,
        gate_expert[:, 0, :],
        up_expert[:, 0, :],
        down_expert[:, 0, :],
    )
    partial_value = partial_value.at[slot_rows].add(values)
    summed = sum_at_owner(partial_value.astype(jnp.bfloat16), "seq", 0)
    layer_out = (merged.astype(jnp.float32) + summed).astype(jnp.bfloat16)
    return layer_out[None]


def solution(mesh):
    placed = (
        P("fsdp", None, None),
        P("fsdp", None),
        P("fsdp", None),
        P("fsdp", "seq", None),
        P("fsdp", None, None),
        P("fsdp", None, None),
        P(),
        P("fsdp", "seq"),
        P("fsdp", "seq"),
        P(),
        P("fsdp", "seq"),
        P(),
        P("fsdp", "seq"),
        P("fsdp", "seq"),
        P("fsdp", "seq"),
        P("fsdp", "seq", None),
        P("fsdp", "seq", None),
        P("fsdp", "seq", None),
    )
    return jax.shard_map(
        shards, mesh=mesh, in_specs=placed, out_specs=P("fsdp", "seq", None), check_vma=False
    )
```

profile of v0, /device:TPU:0, one launch (start us, length us, event | category | flops | bytes accessed | tf_op | source)
XLA Modules:
  0.0 584.5 jit_solution(8994324096411990108)
XLA Ops:
  6.5 1.7 pad_maximum_fusion
  8.3 3.2 convert_reduce_fusion
  12.1 1.4 multiply_reduce_fusion.1
  13.5 33.0 %all-gather.7.cloned.1.call-done = bf16[1152,1076]{1,0:T(8,128)(2,1)} async-done(((bf16[72,1076]{1,0:T(8,128)(2,1)}), bf16[1152,1076]{1,0:T(8,128)(2,1)}) %all-gather.7.cloned.1.call-update) | async-done | bytes 2479120 | tf_op jit(solution)/shard_map/all_gather | solution.py:12
  46.5 13.0 %convolution_convert_fusion = bf16[2048,1152]{1,0:T(8,128)(2,1)} fusion(bf16[1152,1076]{1,0:T(8,128)(2,1)} %all-gather.7.cloned.1.call-done, bf16[1,2048,1152]{2,1,0:T(8,128)(2,1)} %param.18, f32[1152]{0:T(1024)S(1)} %copy-done.13, f32[2048]{0:T(1024)S(1)} %add_rsqrt_fusion, f32[2048]{0:T(1024)S(1)} %broadcast_multiply_fusion), kind=kOutput, calls=%fused_computation.15 | convolution fusion | flops 5101277184 | bytes 12407296 | tf_op jit(solution)/shard_map/dot_general | solution.py:131
  59.5 88.6 %reduce-scatter.2.cloned.1.call-done = bf16[256,1152]{1,0:T(8,128)(2,1)} async-done(((bf16[2048,1152]{1,0:T(8,128)(2,1)}), bf16[256,1152]{1,0:T(8,128)(2,1)}) %reduce-scatter.2.cloned.1.call-update) | async-done | bytes 589840 | tf_op jit(solution)/shard_map/reduce_scatter | solution.py:26
  148.7 8.6 %reshape.281 = f32[512,4608]{1,0:T(8,128)} reshape(bf16[1,2048,1152]{2,1,0:T(8,128)(2,1)} %param.18) | data formatting | bytes 14155776 | tf_op jit(solution)/shard_map/convert_element_type | solution.py:126
  157.6 1.1 reduce-window.20
  159.2 65.9 %all-gather.15.cloned.1.call-done = bf16[2048,1152]{1,0:T(8,128)(2,1)} async-done(((bf16[256,1152]{1,0:T(8,128)(2,1)}), bf16[2048,1152]{1,0:T(8,128)(2,1)}) %all-gather.15.cloned.1.call-update) | async-done | bytes 4718608 | tf_op jit(solution)/shard_map/all_gather | solution.py:29
  225.0 5.1 fusion
  230.8 5.8 multiply_reduce_fusion
  237.1 8.6 %reshape.282 = f32[512,4608]{1,0:T(8,128)} reshape(bf16[2048,1152]{1,0:T(8,128)(2,1)} %all-gather.15.cloned.1.call-done) | data formatting | bytes 14155776 | tf_op jit(solution)/shard_map/convert_element_type | solution.py:134
  245.7 13.3 %all-gather.9.cloned.1.call-done = bf16[4608,256]{1,0:T(8,128)(2,1)} async-done(((bf16[288,256]{1,0:T(8,128)(2,1)}), bf16[4608,256]{1,0:T(8,128)(2,1)}) %all-gather.9.cloned.1.call-update) | async-done | bytes 2359312 | tf_op jit(solution)/shard_map/all_gather | solution.py:124
  259.0 8.6 %fusion.49 = bf16[512,256]{1,0:T(8,128)(2,1)S(1)} fusion(bf16[4608,256]{1,0:T(8,128)(2,1)} %all-gather.9.cloned.1.call-done, f32[512,4608]{1,0:T(8,128)} %reshape.281, f32[512,4608]{1,0:T(8,128)} %reshape.282, f32[4608]{0:T(1024)S(1)} %copy-done.10, f32[512]{0:T(512)S(1)} %add_rsqrt_fusion.1, f32[512]{0:T(512)S(1)} %broadcast_multiply_fusion.1), kind=kOutput, calls=%fused_computation.53 | convolution fusion | flops 1219887104 | bytes 21518336 | tf_op jit(solution)/shard_map/dot_general | solution.py:138
  267.6 3.1 scatter_custom_fusion.1
  270.7 6.4 %all-to-all-start = ((bf16[8,128,256]{2,1,0:T(8,128)(2,1)}), bf16[8,128,256]{2,1,0:T(8,128)(2,1)S(1)}, u32[]{:S(2)}, u32[]{:S(2)}) async-start(bf16[8,128,256]{2,1,0:T(8,128)(2,1)} %bitcast.15), calls=%async_computation.1 | async-start | bytes 1048576 | tf_op jit(solution)/shard_map/all_to_all | solution.py:148
  277.2 2.4 scatter_custom_fusion
  279.7 8.7 %all-to-all-done = bf16[8,128,256]{2,1,0:T(8,128)(2,1)S(1)} async-done(((bf16[8,128,256]{2,1,0:T(8,128)(2,1)}), bf16[8,128,256]{2,1,0:T(8,128)(2,1)S(1)}, u32[]{:S(2)}, u32[]{:S(2)}) %all-to-all-start) | async-done | bytes 524320 | tf_op jit(solution)/shard_map/all_to_all | solution.py:148
  288.6 1.6 scatter_fusion
  291.9 2.7 concatenate.7
  295.4 4.3 scatter_custom_fusion.3
  299.8 1.1 gather_fusion.1
  302.2 57.9 %all-gather.11.cloned.1.call-done = bf16[1024,2048]{1,0:T(8,128)(2,1)} async-done(((bf16[128,2048]{1,0:T(8,128)(2,1)}), bf16[1024,2048]{1,0:T(8,128)(2,1)}) %all-gather.11.cloned.1.call-update) | async-done | bytes 4194320 | tf_op jit(solution)/shard_map/all_gather | solution.py:164
  360.1 4.2 gather_fusion
  364.3 111.6 %all-gather.13.cloned.1.call-done = bf16[2048,5280]{1,0:T(8,128)(2,1)} async-done(((bf16[128,5280]{1,0:T(8,128)(2,1)}), bf16[2048,5280]{1,0:T(8,128)(2,1)}) %all-gather.13.cloned.1.call-update) | async-done | bytes 21626896 | tf_op jit(solution)/shard_map/all_gather | solution.py:36
  475.9 4.4 fusion.35
  480.2 11.5 %fusion.31 = f32[1024,2048]{1,0:T(8,128)} fusion(bf16[2048,5280]{1,0:T(8,128)(2,1)} %all-gather.13.cloned.1.call-done, bf16[1024,2048]{1,0:T(8,128)(2,1)} %all-gather.11.cloned.1.call-done, f32[1024,352]{0,1:T(8,128)S(1)} %fusion.35), kind=kOutput, calls=%fused_computation.40 | convolution fusion | flops 2954952704 | bytes 17170432 | tf_op jit(solution)/shard_map/dot_general | solution.py:171
  491.7 4.8 fusion.5
  496.5 9.0 %fusion.23 = f32[128,2048]{1,0:T(8,128)S(1)} fusion(bf16[2048,5280]{1,0:T(8,128)(2,1)} %all-gather.13.cloned.1.call-done, f32[128,1408]{1,0:T(8,128)S(1)} %fusion.5, f32[128]{0:T(128)S(1)} %get-tuple-element.5, bf16[128,2048]{1,0:T(8,128)(2,1)S(1)} %gather_fusion, pred[128]{0:T(512)(128)(4,1)S(1)} %get-tuple-element.6), kind=kOutput, calls=%fused_computation.38 | convolution fusion | flops 1478000640 | bytes 13828736 | tf_op jit(solution)/shard_map/dot_general | solution.py:93
  505.5 8.8 %scatter_fusion.1 = f32[1024,2048]{1,0:T(8,128)} fusion(f32[1024,2048]{1,0:T(8,128)} %fusion.31, s32[128]{0:T(128)S(1)} %compare_select_fusion.8, f32[128,2048]{1,0:T(8,128)S(1)} %fusion.23), kind=kCustom, calls=%fused_computation.6 | custom fusion | flops 262144 | bytes 3146240 | tf_op jit(solution)/shard_map/scatter-add | solution.py:187
  514.3 4.0 convert_element_type.110
  518.3 57.5 %all_to_all.20 = bf16[8,128,2048]{2,1,0:T(8,128)(2,1)S(1)} all-to-all(bf16[8,128,2048]{2,1,0:T(8,128)(2,1)S(1)} %bitcast.78), channel_id=1, replica_groups=mesh['seq'=8,'fsdp'=16] {'seq'}, dimensions={0} | all-to-all | bytes 8388608 | tf_op jit(solution)/shard_map/all_to_all | solution.py:52
  (88 shorter events, 8.5 us)
Async XLA Ops:
  6.5 39.9 %all-gather.7.cloned.1.call-start = ((), (), s32[]{:S(2)}) async-start(), calls=%async_computation.3 | async-start | bytes 2820096 | tf_op jit(solution)/shard_map/all_gather | solution.py:12
  8.3 38.2 %copy-start.13 = (f32[1152]{0:T(1024)S(1)}, f32[1152]{0:T(1024)}, u32[]{:S(2)}) copy-start(f32[1152]{0:T(1024)} %param.24) | copy-start | bytes 13828
  8.3 139.8 %reduce-scatter.2.cloned.1.call-start = ((), (), s32[]{:S(2)}) async-start(), calls=%async_computation.4 | async-start | bytes 5308416 | tf_op jit(solution)/shard_map/reduce_scatter | solution.py:26
  8.3 3.8 copy-start
  59.5 165.6 %all-gather.15.cloned.1.call-start = ((), (), s32[]{:S(2)}) async-start(), calls=%async_computation.8 | async-start | bytes 5308416 | tf_op jit(solution)/shard_map/all_gather | solution.py:29
  148.1 110.9 %all-gather.9.cloned.1.call-start = ((), (), s32[]{:S(2)}) async-start(), calls=%async_computation.5 | async-start | bytes 2506752 | tf_op jit(solution)/shard_map/all_gather | solution.py:124
  148.7 8.7 %copy-start.14 = (s32[1,8]{1,0:T(1,128)S(1)}, s32[1,8]{1,0:T(1,128)}, u32[]{:S(2)}) copy-start(s32[1,8]{1,0:T(1,128)} %param.19) | copy-start | bytes 100
  148.7 8.8 %copy-start.12 = (s32[1,8]{1,0:T(1,128)S(1)}, s32[1,8]{1,0:T(1,128)}, u32[]{:S(2)}) copy-start(s32[1,8]{1,0:T(1,128)} %param.20) | copy-start | bytes 100
  237.1 21.9 %copy-start.10 = (f32[4608]{0:T(1024)S(1)}, f32[4608]{0:T(1024)}, u32[]{:S(2)}) copy-start(f32[4608]{0:T(1024)} %param.27) | copy-start | bytes 55300
  267.6 20.9 %copy-start.1 = (bf16[1,128,2048]{2,1,0:T(8,128)(2,1)S(1)}, bf16[1,128,2048]{2,1,0:T(8,128)(2,1)}, u32[]{:S(2)}) copy-start(bf16[1,128,2048]{2,1,0:T(8,128)(2,1)} %param.21) | copy-start | bytes 1572868
  270.7 17.7 %all-to-all-start = ((bf16[8,128,256]{2,1,0:T(8,128)(2,1)}), bf16[8,128,256]{2,1,0:T(8,128)(2,1)S(1)}, u32[]{:S(2)}, u32[]{:S(2)}) async-start(bf16[8,128,256]{2,1,0:T(8,128)(2,1)} %bitcast.15), calls=%async_computation.1 | async-start | bytes 1048576 | tf_op jit(solution)/shard_map/all_to_all | solution.py:148
  277.2 82.9 %all-gather.11.cloned.1.call-start = ((), (), s32[]{:S(2)}) async-start(), calls=%async_computation.6 | async-start | bytes 4718592 | tf_op jit(solution)/shard_map/all_gather | solution.py:164
  288.5 1.9 copy-start.11
  288.5 3.0 copy-start.6
  288.5 3.1 copy-start.7
  288.5 3.2 copy-start.8
  288.5 3.4 copy-start.2
  288.5 3.4 copy-start.3
  288.6 3.4 copy-start.4
  290.2 4.5 copy-start.5
  290.2 9.5 %copy-start.9 = (f32[1,1024,6]{1,0,2:T(1,128)S(1)}, f32[1,1024,6]{1,0,2:T(1,128)}, u32[]{:S(2)}) copy-start(f32[1,1024,6]{1,0,2:T(1,128)} %param.23) | copy-start | bytes 73732
  291.4 184.4 %all-gather.13.cloned.1.call-start = ((), (), s32[]{:S(2)}) async-start(), calls=%async_computation.7 | async-start | bytes 23396352 | tf_op jit(solution)/shard_map/all_gather | solution.py:36
Sparse Core Ops, SparseCore 0:
  9.0 37.3 all-gather.6
  59.6 88.4 reduce-scatter.1
  150.4 74.6 all-gather.14
  226.6 32.3 all-gather.8
  291.6 68.4 all-gather.10
  361.6 114.1 all-gather.12
where the time goes:
time: 591 us; the launch traced here: 585 us
  waiting for transfers between devices  379 us (64%)
  blocking collectives  57.5 us (10%)
  matrix products  51.2 us (9%)
  local copies, waits for them, and re-layouts  39.1 us (7%)
  other arithmetic  36.5 us (6%)
  between operations  14.1 us (2%)
  starting transfers between devices  7.09 us (1%)
    all_gather x1, waiting for transfers between devices, in_one_piece(): lax.all_gather(both, axis, axis=dim, tiled=True)  112 us
    reduce_scatter x1, waiting for transfers between devices, sum_in_two_steps(): lax.psum_scatter(rows_for(lines, lax.axis_size(axis)), axis, scatter_dime...  88.6 us
    all_gather x1, waiting for transfers between devices, sum_in_two_steps(): whole = lax.all_gather(own, axis).reshape(-1, *lines.shape[1:])  65.9 us
    all_gather x1, waiting for transfers between devices, shards(): gathered = lax.all_gather(normed_tokens, 'seq', axis=0, tiled=True)  57.9 us
    all_to_all x1, blocking collectives, sum_at_owner(): parts = lax.all_to_all(split_up(x, dim, count), axis, 0, 0, tiled=True)  57.5 us
    all_gather x1, waiting for transfers between devices, sent_together(): lax.all_gather(both, axis, axis=dim, tiled=True)  33 us
    all_gather x1, waiting for transfers between devices, shards(): lax.all_gather(proj_weight, 'fsdp', axis=0, tiled=True)  13.3 us
    dot_general x1, matrix products, shards(): lax.dot_general(hidden, vit_second, (((1,), (1,)), ((), ())), preferred_e...  13 us
  transfers between devices with their start and end apart: 7, of which 7 were waited for; matrix products, arithmetic and copies ran while one was open for 9% of the time, Pallas kernels for 0%

commit v1 on v0

--- a/solution.py
+++ b/solution.py
@@ -161,7 +161,8 @@
     )
     merged = embeds[0].at[slot_place].set(received[0], mode="drop")
     normed_tokens = rms_norm(merged.astype(jnp.float32), moe_gain).astype(jnp.bfloat16)
-    gathered = lax.all_gather(normed_tokens, "seq", axis=0, tiled=True)
+    stack = jnp.stack([normed_tokens] * lax.axis_size("seq"))
+    gathered = jnp.concatenate(lax.all_to_all(stack, "seq", 0, 0), axis=0)
     gate_shared, up_shared, down_shared, gate_expert, up_expert, down_expert = in_one_piece(
         (shared_gate, shared_up, shared_down, expert_gate, expert_up, expert_down), "fsdp", 0, 1
     )

time: 591 us -> 541 us (0.915)
  waiting for transfers between devices: 379 us -> 323 us
    all_gather x1 -> x0, waiting for transfers between devices: 57.9 us -> none  [shards(): gathered = lax.all_gather(normed_tokens, 'seq', axis=0, tiled=True)]
    all_to_all x0 -> x1, waiting for transfers between devices: none -> 53.3 us  [shards(): gathered = jnp.concatenate(lax.all_to_all(stack, 'seq', 0, 0), axis=0)]
    all_gather x1, waiting for transfers between devices: 112 us -> 62.9 us  [in_one_piece(): lax.all_gather(both, axis, axis=dim, tiled=True)]
  transfers between devices with their start and end apart: 7 -> 7, of which waited for: 7 -> 7; matrix products, arithmetic and copies ran while one was open for 9% -> 13% of each run, Pallas kernels for 0% -> 0%
where the time goes in v1:
time: 541 us; the launch traced here: 535 us
  waiting for transfers between devices  323 us (60%)
  blocking collectives  57.2 us (11%)
  matrix products  51.2 us (9%)
  local copies, waits for them, and re-layouts  42.3 us (8%)
  other arithmetic  35.7 us (7%)
  between operations  13.8 us (3%)
  starting transfers between devices  11.8 us (2%)
    reduce_scatter x1, waiting for transfers between devices, sum_in_two_steps(): lax.psum_scatter(rows_for(lines, lax.axis_size(axis)), axis, scatter_dime...  88.6 us
    all_gather x1, waiting for transfers between devices, in_one_piece(): lax.all_gather(both, axis, axis=dim, tiled=True)  62.9 us
    all_gather x1, waiting for transfers between devices, sum_in_two_steps(): whole = lax.all_gather(own, axis).reshape(-1, *lines.shape[1:])  62 us
    all_to_all x1, blocking collectives, sum_at_owner(): parts = lax.all_to_all(split_up(x, dim, count), axis, 0, 0, tiled=True)  57.2 us
    all_to_all x1, waiting for transfers between devices, shards(): gathered = jnp.concatenate(lax.all_to_all(stack, 'seq', 0, 0), axis=0)  53.3 us
    all_gather x1, waiting for transfers between devices, sent_together(): lax.all_gather(both, axis, axis=dim, tiled=True)  33 us
    all_gather x1, waiting for transfers between devices, shards(): lax.all_gather(proj_weight, 'fsdp', axis=0, tiled=True)  13.3 us
    dot_general x1, matrix products, shards(): lax.dot_general(hidden, vit_second, (((1,), (1,)), ((), ())), preferred_e...  13 us
  transfers between devices with their start and end apart: 7, of which 7 were waited for; matrix products, arithmetic and copies ran while one was open for 13% of the time, Pallas kernels for 0%

profile of v1, /device:TPU:0, one launch (start us, length us, event | category | flops | bytes accessed | tf_op | source)
XLA Modules:
  0.0 535.0 jit_solution(17160019162314684586)
XLA Ops:
  6.5 1.7 pad_maximum_fusion
  8.3 3.2 convert_reduce_fusion
  12.1 1.4 multiply_reduce_fusion.1
  13.5 33.0 %all-gather.6.cloned.1.call-done = bf16[1152,1076]{1,0:T(8,128)(2,1)} async-done(((bf16[72,1076]{1,0:T(8,128)(2,1)}), bf16[1152,1076]{1,0:T(8,128)(2,1)}) %all-gather.6.cloned.1.call-update) | async-done | bytes 2479120 | tf_op jit(solution)/shard_map/all_gather | solution.py:12
  46.5 13.0 %convolution_convert_fusion = bf16[2048,1152]{1,0:T(8,128)(2,1)} fusion(bf16[1152,1076]{1,0:T(8,128)(2,1)} %all-gather.6.cloned.1.call-done, bf16[1,2048,1152]{2,1,0:T(8,128)(2,1)} %param.18, f32[1152]{0:T(1024)S(1)} %copy-done.13, f32[2048]{0:T(1024)S(1)} %add_rsqrt_fusion, f32[2048]{0:T(1024)S(1)} %broadcast_multiply_fusion), kind=kOutput, calls=%fused_computation.15 | convolution fusion | flops 5101277184 | bytes 12407296 | tf_op jit(solution)/shard_map/dot_general | solution.py:131
  59.6 88.6 %reduce-scatter.2.cloned.1.call-done = bf16[256,1152]{1,0:T(8,128)(2,1)} async-done(((bf16[2048,1152]{1,0:T(8,128)(2,1)}), bf16[256,1152]{1,0:T(8,128)(2,1)}) %reduce-scatter.2.cloned.1.call-update) | async-done | bytes 589840 | tf_op jit(solution)/shard_map/reduce_scatter | solution.py:26
  149.7 2.7 concatenate.7
  152.4 8.7 %reshape.287 = f32[512,4608]{1,0:T(8,128)} reshape(bf16[1,2048,1152]{2,1,0:T(8,128)(2,1)} %param.18) | data formatting | bytes 14155776 | tf_op jit(solution)/shard_map/convert_element_type | solution.py:126
  163.0 62.0 %all-gather.12.cloned.1.call-done = bf16[2048,1152]{1,0:T(8,128)(2,1)} async-done(((bf16[256,1152]{1,0:T(8,128)(2,1)}), bf16[2048,1152]{1,0:T(8,128)(2,1)}) %all-gather.12.cloned.1.call-update) | async-done | bytes 4718608 | tf_op jit(solution)/shard_map/all_gather | solution.py:29
  225.0 5.1 fusion
  230.8 5.8 %multiply_reduce_fusion = f32[2048]{0:T(1024)S(1)} fusion(bf16[1,2048,1152]{2,1,0:T(8,128)(2,1)} %param.18, bf16[2048,1152]{1,0:T(8,128)(2,1)} %all-gather.12.cloned.1.call-done, f32[2048]{0:T(1024)S(1)} %sub.65), kind=kLoop, calls=%fused_computation.10 | loop fusion | flops 14153728 | bytes 9453568 | tf_op jit(solution)/shard_map/reduce_sum | solution.py:58
  237.0 8.6 %reshape.288 = f32[512,4608]{1,0:T(8,128)} reshape(bf16[2048,1152]{1,0:T(8,128)(2,1)} %all-gather.12.cloned.1.call-done) | data formatting | bytes 14155776 | tf_op jit(solution)/shard_map/convert_element_type | solution.py:134
  245.7 13.3 %all-gather.8.cloned.1.call-done = bf16[4608,256]{1,0:T(8,128)(2,1)} async-done(((bf16[288,256]{1,0:T(8,128)(2,1)}), bf16[4608,256]{1,0:T(8,128)(2,1)}) %all-gather.8.cloned.1.call-update) | async-done | bytes 2359312 | tf_op jit(solution)/shard_map/all_gather | solution.py:124
  258.9 8.6 %fusion.49 = bf16[512,256]{1,0:T(8,128)(2,1)S(1)} fusion(bf16[4608,256]{1,0:T(8,128)(2,1)} %all-gather.8.cloned.1.call-done, f32[512,4608]{1,0:T(8,128)} %reshape.287, f32[512,4608]{1,0:T(8,128)} %reshape.288, f32[4608]{0:T(1024)S(1)} %copy-done.10, f32[512]{0:T(512)S(1)} %add_rsqrt_fusion.1, f32[512]{0:T(512)S(1)} %broadcast_multiply_fusion.1), kind=kOutput, calls=%fused_computation.53 | convolution fusion | flops 1219887104 | bytes 21518336 | tf_op jit(solution)/shard_map/dot_general | solution.py:138
  267.6 3.1 scatter_custom_fusion.1
  270.7 6.4 %all-to-all-start = ((bf16[8,128,256]{2,1,0:T(8,128)(2,1)}), bf16[8,128,256]{2,1,0:T(8,128)(2,1)S(1)}, u32[]{:S(2)}, u32[]{:S(2)}) async-start(bf16[8,128,256]{2,1,0:T(8,128)(2,1)} %bitcast.15), calls=%async_computation.1 | async-start | bytes 1048576 | tf_op jit(solution)/shard_map/all_to_all | solution.py:148
  277.1 2.4 scatter_custom_fusion
  279.6 9.5 %all-to-all-done = bf16[8,128,256]{2,1,0:T(8,128)(2,1)S(1)} async-done(((bf16[8,128,256]{2,1,0:T(8,128)(2,1)}), bf16[8,128,256]{2,1,0:T(8,128)(2,1)S(1)}, u32[]{:S(2)}, u32[]{:S(2)}) %all-to-all-start) | async-done | bytes 524320 | tf_op jit(solution)/shard_map/all_to_all | solution.py:148
  289.6 1.6 scatter_fusion
  291.7 2.5 stack.2
  294.2 4.8 all-to-all-start.1
  299.7 4.3 scatter_custom_fusion.3
  306.5 53.3 %all-to-all-done.1 = bf16[8,128,2048]{2,1,0:T(8,128)(2,1)} async-done(((bf16[8,128,2048]{2,1,0:T(8,128)(2,1)}), bf16[8,128,2048]{2,1,0:T(8,128)(2,1)}, u32[]{:S(2)}, u32[]{:S(2)}) %all-to-all-start.1) | async-done | bytes 4194336 | tf_op jit(solution)/shard_map/all_to_all | solution.py:165
  359.8 4.3 gather_fusion
  364.1 62.9 %all-gather.10.cloned.1.call-done = bf16[2048,5280]{1,0:T(8,128)(2,1)} async-done(((bf16[128,5280]{1,0:T(8,128)(2,1)}), bf16[2048,5280]{1,0:T(8,128)(2,1)}) %all-gather.10.cloned.1.call-update) | async-done | bytes 21626896 | tf_op jit(solution)/shard_map/all_gather | solution.py:36
  427.0 4.4 fusion.35
  431.3 11.5 %fusion.31 = f32[1024,2048]{1,0:T(8,128)} fusion(bf16[2048,5280]{1,0:T(8,128)(2,1)} %all-gather.10.cloned.1.call-done, bf16[1024,2048]{1,0:T(8,128)(2,1)} %bitcast.19, f32[1024,352]{0,1:T(8,128)S(1)} %fusion.35), kind=kOutput, calls=%fused_computation.40 | convolution fusion | flops 2954952704 | bytes 17170432 | tf_op jit(solution)/shard_map/dot_general | solution.py:172
  442.8 4.8 fusion.5
  447.6 9.0 %fusion.23 = f32[128,2048]{1,0:T(8,128)S(1)} fusion(bf16[2048,5280]{1,0:T(8,128)(2,1)} %all-gather.10.cloned.1.call-done, f32[128,1408]{1,0:T(8,128)S(1)} %fusion.5, f32[128]{0:T(128)S(1)} %get-tuple-element.5, bf16[128,2048]{1,0:T(8,128)(2,1)S(1)} %gather_fusion, pred[128]{0:T(512)(128)(4,1)S(1)} %get-tuple-element.6), kind=kOutput, calls=%fused_computation.38 | convolution fusion | flops 1478000640 | bytes 13828736 | tf_op jit(solution)/shard_map/dot_general | solution.py:93
  456.6 8.8 %scatter_fusion.1 = f32[1024,2048]{1,0:T(8,128)} fusion(f32[1024,2048]{1,0:T(8,128)} %fusion.31, s32[128]{0:T(128)S(1)} %compare_select_fusion.8, f32[128,2048]{1,0:T(8,128)S(1)} %fusion.23), kind=kCustom, calls=%fused_computation.6 | custom fusion | flops 262144 | bytes 3146240 | tf_op jit(solution)/shard_map/scatter-add | solution.py:188
  465.4 4.0 convert_element_type.110
  469.4 57.2 %all_to_all.25 = bf16[8,128,2048]{2,1,0:T(8,128)(2,1)S(1)} all-to-all(bf16[8,128,2048]{2,1,0:T(8,128)(2,1)S(1)} %bitcast.75), channel_id=1, replica_groups=mesh['seq'=8,'fsdp'=16] {'seq'}, dimensions={0} | all-to-all | bytes 8388608 | tf_op jit(solution)/shard_map/all_to_all | solution.py:52
  (89 shorter events, 10.8 us)
Async XLA Ops:
  6.5 39.9 %all-gather.6.cloned.1.call-start = ((), (), s32[]{:S(2)}) async-start(), calls=%async_computation.4 | async-start | bytes 2820096 | tf_op jit(solution)/shard_map/all_gather | solution.py:12
  8.3 38.2 %copy-start.13 = (f32[1152]{0:T(1024)S(1)}, f32[1152]{0:T(1024)}, u32[]{:S(2)}) copy-start(f32[1152]{0:T(1024)} %param.24) | copy-start | bytes 13828
  8.3 139.8 %reduce-scatter.2.cloned.1.call-start = ((), (), s32[]{:S(2)}) async-start(), calls=%async_computation.5 | async-start | bytes 5308416 | tf_op jit(solution)/shard_map/reduce_scatter | solution.py:26
  8.3 3.8 copy-start
  59.4 89.8 %copy-start.6 = (bf16[128,352]{0,1:T(8,128)(2,1)S(1)}, bf16[128,352]{0,1:T(8,128)(2,1)}, u32[]{:S(2)}) copy-start(bf16[128,352]{0,1:T(8,128)(2,1)} %param.30) | copy-start | bytes 270340
  59.4 89.9 %copy-start.7 = (bf16[128,352]{0,1:T(8,128)(2,1)S(1)}, bf16[128,352]{0,1:T(8,128)(2,1)}, u32[]{:S(2)}) copy-start(bf16[128,352]{0,1:T(8,128)(2,1)} %param.31) | copy-start | bytes 270340
  59.4 90.1 %copy-start.8 = (bf16[128,352]{0,1:T(8,128)(2,1)S(1)}, bf16[128,352]{0,1:T(8,128)(2,1)}, u32[]{:S(2)}) copy-start(bf16[128,352]{0,1:T(8,128)(2,1)} %param.32) | copy-start | bytes 270340
  59.4 90.2 %copy-start.2 = (bf16[128,1,1408]{2,0,1:T(8,128)(2,1)S(1)}, bf16[128,1,1408]{2,0,1:T(8,128)(2,1)}, u32[]{:S(2)}) copy-start(bf16[128,1,1408]{2,0,1:T(8,128)(2,1)} %param.33) | copy-start | bytes 1081348
  59.5 90.2 %copy-start.3 = (bf16[128,1,1408]{2,0,1:T(8,128)(2,1)S(1)}, bf16[128,1,1408]{2,0,1:T(8,128)(2,1)}, u32[]{:S(2)}) copy-start(bf16[128,1,1408]{2,0,1:T(8,128)(2,1)} %param.34) | copy-start | bytes 1081348
  59.5 90.2 %copy-start.4 = (bf16[128,1,1408]{2,0,1:T(8,128)(2,1)S(1)}, bf16[128,1,1408]{2,0,1:T(8,128)(2,1)}, u32[]{:S(2)}) copy-start(bf16[128,1,1408]{2,0,1:T(8,128)(2,1)} %param.35) | copy-start | bytes 1081348
  59.5 165.5 %all-gather.12.cloned.1.call-start = ((), (), s32[]{:S(2)}) async-start(), calls=%async_computation.8 | async-start | bytes 5308416 | tf_op jit(solution)/shard_map/all_gather | solution.py:29
  148.1 110.8 %all-gather.8.cloned.1.call-start = ((), (), s32[]{:S(2)}) async-start(), calls=%async_computation.6 | async-start | bytes 2506752 | tf_op jit(solution)/shard_map/all_gather | solution.py:124
  148.7 278.3 %all-gather.10.cloned.1.call-start = ((), (), s32[]{:S(2)}) async-start(), calls=%async_computation.7 | async-start | bytes 23396352 | tf_op jit(solution)/shard_map/all_gather | solution.py:36
  152.4 8.7 %copy-start.14 = (s32[1,8]{1,0:T(1,128)S(1)}, s32[1,8]{1,0:T(1,128)}, u32[]{:S(2)}) copy-start(s32[1,8]{1,0:T(1,128)} %param.19) | copy-start | bytes 100
  152.4 8.9 %copy-start.12 = (s32[1,8]{1,0:T(1,128)S(1)}, s32[1,8]{1,0:T(1,128)}, u32[]{:S(2)}) copy-start(s32[1,8]{1,0:T(1,128)} %param.20) | copy-start | bytes 100
  237.0 21.9 %copy-start.10 = (f32[4608]{0:T(1024)S(1)}, f32[4608]{0:T(1024)}, u32[]{:S(2)}) copy-start(f32[4608]{0:T(1024)} %param.27) | copy-start | bytes 55300
  267.6 22.1 %copy-start.1 = (bf16[1,128,2048]{2,1,0:T(8,128)(2,1)S(1)}, bf16[1,128,2048]{2,1,0:T(8,128)(2,1)}, u32[]{:S(2)}) copy-start(bf16[1,128,2048]{2,1,0:T(8,128)(2,1)} %param.21) | copy-start | bytes 1572868
  270.7 18.4 %all-to-all-start = ((bf16[8,128,256]{2,1,0:T(8,128)(2,1)}), bf16[8,128,256]{2,1,0:T(8,128)(2,1)S(1)}, u32[]{:S(2)}, u32[]{:S(2)}) async-start(bf16[8,128,256]{2,1,0:T(8,128)(2,1)} %bitcast.15), calls=%async_computation.1 | async-start | bytes 1048576 | tf_op jit(solution)/shard_map/all_to_all | solution.py:148
  289.6 1.8 copy-start.11
  294.2 4.8 copy-start.5
  294.2 9.8 %copy-start.9 = (f32[1,1024,6]{1,0,2:T(1,128)S(1)}, f32[1,1024,6]{1,0,2:T(1,128)}, u32[]{:S(2)}) copy-start(f32[1,1024,6]{1,0,2:T(1,128)} %param.23) | copy-start | bytes 73732
  294.2 65.6 %all-to-all-start.1 = ((bf16[8,128,2048]{2,1,0:T(8,128)(2,1)}), bf16[8,128,2048]{2,1,0:T(8,128)(2,1)}, u32[]{:S(2)}, u32[]{:S(2)}) async-start(bf16[8,128,2048]{2,1,0:T(8,128)(2,1)} %stack.2), calls=%async_computation.2 | async-start | bytes 8388608 | tf_op jit(solution)/shard_map/all_to_all | solution.py:165
Sparse Core Ops, SparseCore 0:
  9.0 37.3 all-gather.5
  59.6 88.4 reduce-scatter.1
  150.4 74.5 all-gather.11
  226.6 32.3 all-gather.7
  260.5 166.4 all-gather.9
